TPU v7x, 32 devices: a whole 2x2x4 slice. The times are simulated.
32 devices in a mesh: grp: 4 (over y, x), lane: 8 (over z, core).
Axes of the slice: x: 2, y: 2, z: 4, core: 2. Of those that a mesh axis runs over, the one named last changes fastest.
Arguments:
- ctrl_factor: bfloat16 [49152, 512], P(('grp', 'lane')), may hold values from -6 to 6
- obs_factor: bfloat16 [49152, 512], P(('grp', 'lane')), may hold values from -6 to 6
- block_cols: int32 [384, 4], P(('grp', 'lane')), may hold values from -1 to 383, as said below
- mass_blocks: bfloat16 [384, 4, 128, 128], P(('grp', 'lane')), may hold values from -0.25 to 0.25
Outputs:
- cross_gram: float32 [512, 512], P('lane')
Inputs may be any that keep to these rules, and one draw needn't show every extreme that they name: block_cols[g, 0] is g; every other entry is -1 or a block index within 2 of g, distinct within a row; row block 0 has an empty slot.
All inputs are finite; a program needn't handle non-finite values.
Results may differ from a plain program's by a relative error of at most 0.0029.
Values may be sent and summed in bfloat16 or wider, within the bound.
A program may use at most 64 MiB of HBM per device.

v0:
```python
import functools

import jax
import jax.numpy as jnp
from jax import lax
from jax.experimental import pallas as pl
from jax.experimental.pallas import tpu as pltpu
from jax.sharding import PartitionSpec as P

MESH = pl.DeviceIdType.MESH
F32 = jnp.float32
BF16 = jnp.bfloat16
CORES = 2
CHUNKS = 2


def row_order(width, lanes, groups, fused):
    if not fused:
        return [(0, 0, width)]
    zs = lanes // CORES
    piece = width // (lanes * groups)
    order = []
    for core in range(CORES):
        for q in range(groups):
            for z in range(zs):
                source = (z * CORES + core) * (width // lanes) + q * piece
                order.append((source, ((core * groups + q) * zs + z) * piece, piece))
    return order


def kernel(
    groups, lanes, fused, nblk, bs, cols_hbm, ctrl_hbm, obs_hbm, mass_hbm, out_ref,
    cols_ref, ctrl_v, obs_v, mass_v, band, obs_in, obs_edge, mc_in, mc_edge, gram,
    send_a, recv_a, send_b, recv_b, send_c, recv_c, gath,
    load_sem, hs_sem, hr_sem, as_sem, ar_sem, bs_sem, br_sem, cs_sem, cr_sem, ds_sem, dr_sem,
):
    q = lax.axis_index("grp")
    lane = lax.axis_index("lane")
    zs = lanes // CORES
    core = lax.rem(lane, CORES)
    z = lane // CORES
    me = q * lanes + lane
    last = groups * lanes - 1
    rows = nblk * bs
    halo = 2 * bs
    width = ctrl_v.shape[1]

    loads = [
        pltpu.make_async_copy(ctrl_hbm, ctrl_v.at[pl.ds(halo, rows)], load_sem.at[0]),
        pltpu.make_async_copy(mass_hbm, mass_v, load_sem.at[1]),
        pltpu.make_async_copy(obs_hbm, obs_v, load_sem.at[2]),
        pltpu.make_async_copy(cols_hbm, cols_ref, load_sem.at[3]),
    ]
    def place(index):
        return (index // lanes, lax.rem(index, lanes))

    def grp_peer(k):
        return (lax.rem(q + k, groups), lane)

    def turn(i):
        return i + (1 - lax.rem(q, 2)) * (groups - 2 * i)

    def z_peer(k):
        return (q, lax.rem(z + k, zs) * CORES + core)

    partner = (q, lane + 1 - 2 * core)
    barrier = pltpu.get_barrier_semaphore()

    @pl.when(me > 0)
    def _():
        pl.semaphore_signal(barrier, inc=1, device_id=place(me - 1), device_id_type=MESH)

    @pl.when(me < last)
    def _():
        pl.semaphore_signal(barrier, inc=1, device_id=place(me + 1), device_id_type=MESH)

    peers = 0
    if fused:
        pl.semaphore_signal(barrier, inc=1, device_id=partner, device_id_type=MESH)
        for k in range(1, groups):
            pl.semaphore_signal(barrier, inc=1, device_id=grp_peer(k), device_id_type=MESH)
        for k in range(1, zs):
            pl.semaphore_signal(barrier, inc=1, device_id=z_peer(k), device_id_type=MESH)
        peers = groups + zs - 1

    for load in loads:
        load.start()

    @pl.when((me > 0) & (me < last))
    def _():
        pl.semaphore_wait(barrier, peers + 2)

    @pl.when((me == 0) | (me == last))
    def _():
        pl.semaphore_wait(barrier, peers + 1)

    chunk = width // CHUNKS
    chunks = [slice(h * chunk, (h + 1) * chunk) for h in range(CHUNKS)]

    def to_left(h):
        return pltpu.make_async_remote_copy(
            src_ref=ctrl_v.at[pl.ds(halo, halo), chunks[h]],
            dst_ref=ctrl_v.at[pl.ds(halo + rows, halo), chunks[h]],
            send_sem=hs_sem.at[0, h],
            recv_sem=hr_sem.at[1, h],
            device_id=place(me - 1),
            device_id_type=MESH,
        )

    def to_right(h):
        return pltpu.make_async_remote_copy(
            src_ref=ctrl_v.at[pl.ds(rows, halo), chunks[h]],
            dst_ref=ctrl_v.at[pl.ds(0, halo), chunks[h]],
            send_sem=hs_sem.at[1, h],
            recv_sem=hr_sem.at[0, h],
            device_id=place(me + 1),
            device_id_type=MESH,
        )

    loads[0].wait()

    for h in range(CHUNKS):
        @pl.when(me > 0)
        def _():
            to_left(h).start()

        @pl.when(me < last)
        def _():
            to_right(h).start()

    @pl.when(me == 0)
    def _():
        ctrl_v[pl.ds(0, halo), :] = jnp.zeros((halo, width), BF16)

    @pl.when(me == last)
    def _():
        ctrl_v[pl.ds(halo + rows, halo), :] = jnp.zeros((halo, width), BF16)

    pairs = nblk // 2
    zero = jnp.zeros((bs, bs), BF16)
    slots = mass_v.shape[1]

    def build(p):
        for j in range(2):
            g = 2 * p + j
            offsets = []
            for s in range(1, slots):
                col = cols_ref[s, g]
                offsets.append(jnp.where(col >= 0, col - (me * nblk + g), 99))
            for b in range(6):
                d = b - 2 - j
                if d == 0:
                    block = mass_v[g, 0]
                elif abs(d) > 2:
                    block = zero
                else:
                    block = zero
                    for s in range(1, slots):
                        block = jnp.where(offsets[s - 1] == d, mass_v[g, s], block)
                band[p, j * bs:(j + 1) * bs, b * bs:(b + 1) * bs] = block

    def product(p, cols):
        return jnp.dot(
            band[p], ctrl_v[pl.ds(p * halo, 3 * halo), cols], preferred_element_type=F32
        ).astype(BF16)

    order = row_order(width, lanes, groups, fused)

    def turned(p, target, at):
        block = obs_v[pl.ds(p * halo, halo), :].T
        for source, dest, count in order:
            target[dest:dest + count, at:at + halo] = block[source:source + count, :]

    loads[1].wait()
    loads[3].wait()
    for p in range(1, pairs - 1):
        build(p)
        mc_in[(p - 1) * halo:p * halo, :] = product(p, slice(0, width))
    build(0)
    build(pairs - 1)
    loads[2].wait()
    for p in range(1, pairs - 1):
        turned(p, obs_in, (p - 1) * halo)
    turned(0, obs_edge, 0)
    turned(pairs - 1, obs_edge, halo)
    half = width // 2
    for r in range(2):
        gram[r * half:(r + 1) * half, :] = jnp.dot(
            obs_in[r * half:(r + 1) * half, :], mc_in[...], preferred_element_type=F32
        )

    def edges(h):
        @pl.when(me > 0)
        def _():
            to_right(h).wait_recv()

        mc_edge[0:halo, chunks[h]] = product(0, chunks[h])

        @pl.when(me < last)
        def _():
            to_left(h).wait_recv()

        mc_edge[halo:2 * halo, chunks[h]] = product(pairs - 1, chunks[h])

    def finished(start, count, cols):
        return gram[pl.ds(start, count), cols] + jnp.dot(
            obs_edge[pl.ds(start, count), :], mc_edge[:, cols], preferred_element_type=F32
        )

    def halo_sent():
        for h in range(CHUNKS):
            @pl.when(me > 0)
            def _():
                to_left(h).wait_send()

            @pl.when(me < last)
            def _():
                to_right(h).wait_send()

    if not fused:
        for h in range(CHUNKS):
            edges(h)
        out_ref[...] = finished(0, width, slice(0, width))
        halo_sent()
        return

    theirs = pl.multiple_of((1 - core) * half, half)
    mine = pl.multiple_of(core * half, half)
    copies_a, copies_b, copies_c, copies_d = [], [], [], []
    part = half // groups

    def copy_b(h, k):
        return pltpu.make_async_remote_copy(
            src_ref=send_b.at[h, lax.rem(q + k, groups)], dst_ref=recv_b.at[h, k - 1],
            send_sem=bs_sem.at[h, k - 1], recv_sem=br_sem.at[h, k - 1],
            device_id=grp_peer(k), device_id_type=MESH,
        )

    def copy_d(h, k):
        return pltpu.make_async_remote_copy(
            src_ref=gath.at[h, q], dst_ref=gath.at[h, q],
            send_sem=ds_sem.at[h, k - 1], recv_sem=dr_sem.at[h, k - 1],
            device_id=grp_peer(k), device_id_type=MESH,
        )

    for h, cols in enumerate(chunks):
        edges(h)
        send_a[h] = finished(theirs, half, cols).astype(BF16)
        copy = pltpu.make_async_remote_copy(
            src_ref=send_a.at[h], dst_ref=recv_a.at[h],
            send_sem=as_sem.at[h], recv_sem=ar_sem.at[h],
            device_id=partner, device_id_type=MESH,
        )
        copy.start()
        copies_a.append(copy)
        gram[pl.ds(mine, half), cols] = finished(mine, half, cols)
        copy.wait_recv()

        total = gram[pl.ds(mine, half), cols] + recv_a[h].astype(F32)
        gram[pl.ds(mine, half), cols] = total
        send_b[h] = total.astype(BF16).reshape(groups, part, chunk)
        for i in range(1, groups):
            copy = copy_b(h, turn(i))
            copy.start()
            copies_b.append(copy_b(h, i))

    piece = part // zs
    for h, cols in enumerate(chunks):
        own = gram[pl.ds(pl.multiple_of(core * half + q * part, part), part), cols]
        for k in range(1, groups):
            copies_b[h * (groups - 1) + k - 1].wait_recv()
            own = own + recv_b[h, k - 1].astype(F32)
        gram[0:part, cols] = own
        send_c[h] = own.astype(BF16).reshape(zs, piece, chunk)
        for k in range(1, zs):
            copy = pltpu.make_async_remote_copy(
                src_ref=send_c.at[h, lax.rem(z + k, zs)], dst_ref=recv_c.at[h, k - 1],
                send_sem=cs_sem.at[h, k - 1], recv_sem=cr_sem.at[h, k - 1],
                device_id=z_peer(k), device_id_type=MESH,
            )
            copy.start()
            copies_c.append(copy)

    for h, cols in enumerate(chunks):
        share = gram[pl.ds(pl.multiple_of(z * piece, piece), piece), cols]
        for k in range(1, zs):
            copies_c[h * (zs - 1) + k - 1].wait_recv()
            share = share + recv_c[h, k - 1].astype(F32)
        gath[h, q] = share
        for i in range(1, groups):
            copy = copy_d(h, turn(i))
            copy.start()
            copies_d.append(copy_d(h, i))
    halo_sent()
    for copy in copies_a + copies_b + copies_c:
        copy.wait_send()
    for h, cols in enumerate(chunks):
        for k in range(1, groups):
            copies_d[h * (groups - 1) + k - 1].wait()
        out_ref[:, cols] = gath[h].reshape(out_ref.shape[0], chunk)


def solution(mesh):
    groups, lanes = mesh.shape["grp"], mesh.shape["lane"]

    def shards(ctrl_factor, obs_factor, block_cols, mass_blocks):
        nblk, slots = block_cols.shape
        rows, width = ctrl_factor.shape
        bs = rows // nblk
        halo = 2 * bs
        fused = width % (lanes * groups * 16) == 0
        pairs = nblk // 2
        zs = lanes // CORES
        half, chunk = width // 2, width // CHUNKS
        part = max(half // groups, 16)
        piece = max(part // zs, 16)
        out_rows = width // lanes if fused else width
        dma = pltpu.SemaphoreType.DMA
        result = pl.pallas_call(
            functools.partial(kernel, groups, lanes, fused, nblk, bs),
            out_shape=pltpu.VMEM((out_rows, width), F32),
            in_specs=[pl.BlockSpec(memory_space=pltpu.HBM)] * 4,
            out_specs=pl.BlockSpec(memory_space=pltpu.VMEM),
            scratch_shapes=[
                pltpu.SMEM((slots, nblk), jnp.int32),
                pltpu.VMEM((rows + 2 * halo, width), BF16),
                pltpu.VMEM((rows, width), BF16),
                pltpu.VMEM((nblk, slots, bs, bs), BF16),
                pltpu.VMEM((pairs, halo, 3 * halo), BF16),
                pltpu.VMEM((width, rows - 2 * halo), BF16),
                pltpu.VMEM((width, 2 * halo), BF16),
                pltpu.VMEM((rows - 2 * halo, width), BF16),
                pltpu.VMEM((2 * halo, width), BF16),
                pltpu.VMEM((width, width), F32),
                pltpu.VMEM((CHUNKS, half, chunk), BF16),
                pltpu.VMEM((CHUNKS, half, chunk), BF16),
                pltpu.VMEM((CHUNKS, groups, part, chunk), BF16),
                pltpu.VMEM((CHUNKS, groups - 1, part, chunk), BF16),
                pltpu.VMEM((CHUNKS, zs, piece, chunk), BF16),
                pltpu.VMEM((CHUNKS, zs - 1, piece, chunk), BF16),
                pltpu.VMEM((CHUNKS, groups, piece, chunk), F32),
                dma((4,)), dma((2, CHUNKS)), dma((2, CHUNKS)), dma((CHUNKS,)), dma((CHUNKS,)),
                dma((CHUNKS, groups - 1)), dma((CHUNKS, groups - 1)),
                dma((CHUNKS, zs - 1)), dma((CHUNKS, zs - 1)),
                dma((CHUNKS, groups - 1)), dma((CHUNKS, groups - 1)),
            ],
            compiler_params=pltpu.CompilerParams(
                collective_id=0, has_side_effects=True, vmem_limit_bytes=56 * 2**20
            ),
        )(block_cols.T, ctrl_factor, obs_factor, mass_blocks)
        if fused:
            return result
        share = lax.psum_scatter(result, "lane", scatter_dimension=0, tiled=True)
        return lax.psum(share, "grp")

    placed = (
        P(("grp", "lane"), None),
        P(("grp", "lane"), None),
        P(("grp", "lane"), None),
        P(("grp", "lane"), None, None, None),
    )
    return jax.shard_map(
        shards, mesh=mesh, in_specs=placed, out_specs=P("lane", None), check_vma=False
    )
```

profile of v0, /device:TPU:0, one launch (start us, length us, event | category | flops | bytes accessed | tf_op | source)
XLA Modules:
  0.0 27.4 jit_solution(9762668916807068353)
XLA Ops:
  0.0 26.8 %shard_map.46 = f32[64,512]{1,0:T(8,128)S(1)} custom-call(s32[4,12]{1,0:T(4,128)} %bitcast.1, bf16[1536,512]{1,0:T(8,128)(2,1)} %ctrl_hbm.1, bf16[1536,512]{1,0:T(8,128)(2,1)} %obs_hbm.1, bf16[12,4,128,128]{3,2,1,0:T(8,128)(2,1)} %mass_hbm.1), custom_call_target="tpu_custom_call" | custom-call | tf_op jit(solution)/shard_map/pallas_call | solution.py:319
  26.8 0.7 %copy.6 = f32[64,512]{1,0:T(8,128)} copy(f32[64,512]{1,0:T(8,128)S(1)} %shard_map.46) | data formatting | bytes 262144
where the time goes:
time: 27.6 us; the launch traced here: 27.4 us
  Pallas kernels  26.8 us (97%)
  local copies, waits for them, and re-layouts  0.66 us (2%)
    pallas_call x1, Pallas kernels, shards(): pl.pallas_call(functools.partial(kernel, groups, lanes, fused, nblk, bs),...  26.8 us
    unnamed x1, local copies, waits for them, and re-layouts  0.66 us

commit v1 on v0

--- a/solution.py
+++ b/solution.py
@@ -11,28 +11,26 @@
 F32 = jnp.float32
 BF16 = jnp.bfloat16
 CORES = 2
-CHUNKS = 2
-
-
-def row_order(width, lanes, groups, fused):
+CHUNKS = 4
+
+
+def row_order(width, lanes, fused):
     if not fused:
         return [(0, 0, width)]
     zs = lanes // CORES
-    piece = width // (lanes * groups)
-    order = []
-    for core in range(CORES):
-        for q in range(groups):
-            for z in range(zs):
-                source = (z * CORES + core) * (width // lanes) + q * piece
-                order.append((source, ((core * groups + q) * zs + z) * piece, piece))
-    return order
+    piece = width // lanes
+    return [
+        ((z * CORES + core) * piece, (core * zs + z) * piece, piece)
+        for core in range(CORES)
+        for z in range(zs)
+    ]
 
 
 def kernel(
     groups, lanes, fused, nblk, bs, cols_hbm, ctrl_hbm, obs_hbm, mass_hbm, out_ref,
     cols_ref, ctrl_v, obs_v, mass_v, band, obs_in, obs_edge, mc_in, mc_edge, gram,
-    send_a, recv_a, send_b, recv_b, send_c, recv_c, gath,
-    load_sem, hs_sem, hr_sem, as_sem, ar_sem, bs_sem, br_sem, cs_sem, cr_sem, ds_sem, dr_sem,
+    send_a, recv_a, send_z, recv_z, gath,
+    load_sem, hs_sem, hr_sem, as_sem, ar_sem, zs_sem, zr_sem, gs_sem, gr_sem,
 ):
     q = lax.axis_index("grp")
     lane = lax.axis_index("lane")
@@ -164,7 +162,7 @@
             band[p], ctrl_v[pl.ds(p * halo, 3 * halo), cols], preferred_element_type=F32
         ).astype(BF16)
 
-    order = row_order(width, lanes, groups, fused)
+    order = row_order(width, lanes, fused)
 
     def turned(p, target, at):
         block = obs_v[pl.ds(p * halo, halo), :].T
@@ -226,78 +224,76 @@
 
     theirs = pl.multiple_of((1 - core) * half, half)
     mine = pl.multiple_of(core * half, half)
-    copies_a, copies_b, copies_c, copies_d = [], [], [], []
-    part = half // groups
-
-    def copy_b(h, k):
-        return pltpu.make_async_remote_copy(
-            src_ref=send_b.at[h, lax.rem(q + k, groups)], dst_ref=recv_b.at[h, k - 1],
-            send_sem=bs_sem.at[h, k - 1], recv_sem=br_sem.at[h, k - 1],
-            device_id=grp_peer(k), device_id_type=MESH,
-        )
-
-    def copy_d(h, k):
-        return pltpu.make_async_remote_copy(
-            src_ref=gath.at[h, q], dst_ref=gath.at[h, q],
-            send_sem=ds_sem.at[h, k - 1], recv_sem=dr_sem.at[h, k - 1],
-            device_id=grp_peer(k), device_id_type=MESH,
-        )
-
-    for h, cols in enumerate(chunks):
-        edges(h)
-        send_a[h] = finished(theirs, half, cols).astype(BF16)
-        copy = pltpu.make_async_remote_copy(
+    piece = width // lanes
+
+    def copy_a(h):
+        return pltpu.make_async_remote_copy(
             src_ref=send_a.at[h], dst_ref=recv_a.at[h],
             send_sem=as_sem.at[h], recv_sem=ar_sem.at[h],
             device_id=partner, device_id_type=MESH,
         )
-        copy.start()
-        copies_a.append(copy)
-        gram[pl.ds(mine, half), cols] = finished(mine, half, cols)
-        copy.wait_recv()
-
-        total = gram[pl.ds(mine, half), cols] + recv_a[h].astype(F32)
-        gram[pl.ds(mine, half), cols] = total
-        send_b[h] = total.astype(BF16).reshape(groups, part, chunk)
+
+    def copy_z(h, k):
+        return pltpu.make_async_remote_copy(
+            src_ref=send_z.at[h, lax.rem(z + k, zs)], dst_ref=recv_z.at[h, k - 1],
+            send_sem=zs_sem.at[h, k - 1], recv_sem=zr_sem.at[h, k - 1],
+            device_id=z_peer(k), device_id_type=MESH,
+        )
+
+    def copy_g(h, k):
+        return pltpu.make_async_remote_copy(
+            src_ref=gath.at[h, q], dst_ref=gath.at[h, q],
+            send_sem=gs_sem.at[h, k - 1], recv_sem=gr_sem.at[h, k - 1],
+            device_id=grp_peer(k), device_id_type=MESH,
+        )
+
+    def stage_edges(h):
+        edges(h)
+        send_a[h] = finished(theirs, half, chunks[h])
+        copy_a(h).start()
+        gram[pl.ds(mine, half), chunks[h]] = finished(mine, half, chunks[h])
+
+    def stage_core(h):
+        copy_a(h).wait_recv()
+        total = gram[pl.ds(mine, half), chunks[h]] + recv_a[h]
+        gram[pl.ds(mine, half), chunks[h]] = total
+        send_z[h] = total.astype(BF16).reshape(zs, piece, chunk)
+        for k in range(1, zs):
+            copy_z(h, k).start()
+
+    def stage_z(h):
+        share = gram[pl.ds(pl.multiple_of(core * half + z * piece, piece), piece), chunks[h]]
+        for k in range(1, zs):
+            copy_z(h, k).wait_recv()
+            share = share + recv_z[h, k - 1].astype(F32)
+        gath[h, q] = share.astype(BF16)
         for i in range(1, groups):
-            copy = copy_b(h, turn(i))
-            copy.start()
-            copies_b.append(copy_b(h, i))
-
-    piece = part // zs
-    for h, cols in enumerate(chunks):
-        own = gram[pl.ds(pl.multiple_of(core * half + q * part, part), part), cols]
+            copy_g(h, turn(i)).start()
+
+    def stage_grp(h):
         for k in range(1, groups):
-            copies_b[h * (groups - 1) + k - 1].wait_recv()
-            own = own + recv_b[h, k - 1].astype(F32)
-        gram[0:part, cols] = own
-        send_c[h] = own.astype(BF16).reshape(zs, piece, chunk)
+            copy_g(h, k).wait_recv()
+        total = gath[h, 0].astype(F32)
+        for k in range(1, groups):
+            total = total + gath[h, k].astype(F32)
+        out_ref[:, chunks[h]] = total
+
+    for h in range(CHUNKS):
+        stage_edges(h)
+        if h >= 1:
+            stage_core(h - 1)
+    stage_core(CHUNKS - 1)
+    for h in range(CHUNKS):
+        stage_z(h)
+    for h in range(CHUNKS):
+        stage_grp(h)
+    halo_sent()
+    for h in range(CHUNKS):
+        copy_a(h).wait_send()
         for k in range(1, zs):
-            copy = pltpu.make_async_remote_copy(
-                src_ref=send_c.at[h, lax.rem(z + k, zs)], dst_ref=recv_c.at[h, k - 1],
-                send_sem=cs_sem.at[h, k - 1], recv_sem=cr_sem.at[h, k - 1],
-                device_id=z_peer(k), device_id_type=MESH,
-            )
-            copy.start()
-            copies_c.append(copy)
-
-    for h, cols in enumerate(chunks):
-        share = gram[pl.ds(pl.multiple_of(z * piece, piece), piece), cols]
-        for k in range(1, zs):
-            copies_c[h * (zs - 1) + k - 1].wait_recv()
-            share = share + recv_c[h, k - 1].astype(F32)
-        gath[h, q] = share
-        for i in range(1, groups):
-            copy = copy_d(h, turn(i))
-            copy.start()
-            copies_d.append(copy_d(h, i))
-    halo_sent()
-    for copy in copies_a + copies_b + copies_c:
-        copy.wait_send()
-    for h, cols in enumerate(chunks):
+            copy_z(h, k).wait_send()
         for k in range(1, groups):
-            copies_d[h * (groups - 1) + k - 1].wait()
-        out_ref[:, cols] = gath[h].reshape(out_ref.shape[0], chunk)
+            copy_g(h, k).wait_send()
 
 
 def solution(mesh):
@@ -312,8 +308,7 @@
         pairs = nblk // 2
         zs = lanes // CORES
         half, chunk = width // 2, width // CHUNKS
-        part = max(half // groups, 16)
-        piece = max(part // zs, 16)
+        piece = width // lanes
         out_rows = width // lanes if fused else width
         dma = pltpu.SemaphoreType.DMA
         result = pl.pallas_call(
@@ -332,15 +327,12 @@
                 pltpu.VMEM((rows - 2 * halo, width), BF16),
                 pltpu.VMEM((2 * halo, width), BF16),
                 pltpu.VMEM((width, width), F32),
-                pltpu.VMEM((CHUNKS, half, chunk), BF16),
-                pltpu.VMEM((CHUNKS, half, chunk), BF16),
-                pltpu.VMEM((CHUNKS, groups, part, chunk), BF16),
-                pltpu.VMEM((CHUNKS, groups - 1, part, chunk), BF16),
+                pltpu.VMEM((CHUNKS, half, chunk), F32),
+                pltpu.VMEM((CHUNKS, half, chunk), F32),
                 pltpu.VMEM((CHUNKS, zs, piece, chunk), BF16),
                 pltpu.VMEM((CHUNKS, zs - 1, piece, chunk), BF16),
-                pltpu.VMEM((CHUNKS, groups, piece, chunk), F32),
+                pltpu.VMEM((CHUNKS, groups, piece, chunk), BF16),
                 dma((4,)), dma((2, CHUNKS)), dma((2, CHUNKS)), dma((CHUNKS,)), dma((CHUNKS,)),
-                dma((CHUNKS, groups - 1)), dma((CHUNKS, groups - 1)),
                 dma((CHUNKS, zs - 1)), dma((CHUNKS, zs - 1)),
                 dma((CHUNKS, groups - 1)), dma((CHUNKS, groups - 1)),
             ],

time: 27.6 us -> 24.5 us (0.89)
  Pallas kernels: 26.8 us -> 23.7 us
    pallas_call x1, Pallas kernels: 26.8 us -> 23.7 us  [shards(): pl.pallas_call(functools.partial(kernel, groups, lanes, fused, nblk, bs),...]
where the time goes in v1:
time: 24.5 us; the launch traced here: 24.4 us
  Pallas kernels  23.7 us (97%)
  local copies, waits for them, and re-layouts  0.66 us (3%)
    pallas_call x1, Pallas kernels, shards(): pl.pallas_call(functools.partial(kernel, groups, lanes, fused, nblk, bs),...  23.7 us
    unnamed x1, local copies, waits for them, and re-layouts  0.66 us

profile of v1, /device:TPU:0, one launch (start us, length us, event | category | flops | bytes accessed | tf_op | source)
XLA Modules:
  0.0 24.4 jit_solution(1698713214931187912)
XLA Ops:
  0.0 23.7 %shard_map.46 = f32[64,512]{1,0:T(8,128)S(1)} custom-call(s32[4,12]{1,0:T(4,128)} %bitcast.1, bf16[1536,512]{1,0:T(8,128)(2,1)} %ctrl_hbm.1, bf16[1536,512]{1,0:T(8,128)(2,1)} %obs_hbm.1, bf16[12,4,128,128]{3,2,1,0:T(8,128)(2,1)} %mass_hbm.1), custom_call_target="tpu_custom_call" | custom-call | tf_op jit(solution)/shard_map/pallas_call | solution.py:314
  23.7 0.7 %copy.6 = f32[64,512]{1,0:T(8,128)} copy(f32[64,512]{1,0:T(8,128)S(1)} %shard_map.46) | data formatting | bytes 262144

commit v2 on v1

--- a/solution.py
+++ b/solution.py
@@ -28,9 +28,9 @@
 
 def kernel(
     groups, lanes, fused, nblk, bs, cols_hbm, ctrl_hbm, obs_hbm, mass_hbm, out_ref,
-    cols_ref, ctrl_v, obs_v, mass_v, band, obs_in, obs_edge, mc_in, mc_edge, gram,
+    cols_ref, ctrl_v, obs_v, mass_v, band, obs_in, obs_edge, mc_in, mc_local, mc_edge, gram,
     send_a, recv_a, send_z, recv_z, gath,
-    load_sem, hs_sem, hr_sem, as_sem, ar_sem, zs_sem, zr_sem, gs_sem, gr_sem,
+    load_sem, hs_sem, hr_sem, as_sem, ar_sem, zs_sem, zr_sem, gs_sem, gr_sem, tok_z, tok_g,
 ):
     q = lax.axis_index("grp")
     lane = lax.axis_index("lane")
@@ -72,25 +72,61 @@
     def _():
         pl.semaphore_signal(barrier, inc=1, device_id=place(me + 1), device_id_type=MESH)
 
+    def z_next(step):
+        return (q, lane + step * CORES)
+
+    def grp_near():
+        if groups != 4:
+            return [grp_peer(k) for k in range(1, groups)]
+        return [(q + 1 - 2 * lax.rem(q, 2), lane), (lax.rem(q + 2, groups), lane)]
+
     peers = 0
     if fused:
         pl.semaphore_signal(barrier, inc=1, device_id=partner, device_id_type=MESH)
-        for k in range(1, groups):
-            pl.semaphore_signal(barrier, inc=1, device_id=grp_peer(k), device_id_type=MESH)
-        for k in range(1, zs):
-            pl.semaphore_signal(barrier, inc=1, device_id=z_peer(k), device_id_type=MESH)
-        peers = groups + zs - 1
+        for peer in grp_near():
+            pl.semaphore_signal(barrier, inc=1, device_id=peer, device_id_type=MESH)
+        peers = 1 + len(grp_near())
+
+        @pl.when(z > 0)
+        def _():
+            pl.semaphore_signal(barrier, inc=1, device_id=z_next(-1), device_id_type=MESH)
+
+        @pl.when(z < zs - 1)
+        def _():
+            pl.semaphore_signal(barrier, inc=1, device_id=z_next(1), device_id_type=MESH)
 
     for load in loads:
         load.start()
 
-    @pl.when((me > 0) & (me < last))
-    def _():
-        pl.semaphore_wait(barrier, peers + 2)
-
-    @pl.when((me == 0) | (me == last))
-    def _():
-        pl.semaphore_wait(barrier, peers + 1)
+    lines = 0
+    if fused:
+        lines = (z > 0).astype(jnp.int32) + (z < zs - 1).astype(jnp.int32)
+    ends = (me > 0).astype(jnp.int32) + (me < last).astype(jnp.int32)
+    pl.semaphore_wait(barrier, peers + lines + ends)
+
+    def tell_z(step):
+        @pl.when(z < zs - 1)
+        def _():
+            pl.semaphore_signal(
+                tok_z.at[0, step], inc=1, device_id=z_next(1), device_id_type=MESH
+            )
+
+        @pl.when(z > 0)
+        def _():
+            pl.semaphore_signal(
+                tok_z.at[1, step], inc=1, device_id=z_next(-1), device_id_type=MESH
+            )
+
+    def hear_z(step):
+        @pl.when(z > 0)
+        def _():
+            pl.semaphore_wait(tok_z.at[0, step], 1)
+
+        @pl.when(z < zs - 1)
+        def _():
+            pl.semaphore_wait(tok_z.at[1, step], 1)
+
+    steps = zs - 2 if fused else 0
 
     chunk = width // CHUNKS
     chunks = [slice(h * chunk, (h + 1) * chunk) for h in range(CHUNKS)]
@@ -125,6 +161,12 @@
         @pl.when(me < last)
         def _():
             to_right(h).start()
+
+    if fused:
+        if steps > 0:
+            tell_z(0)
+        if groups == 4:
+            pl.semaphore_signal(tok_g, inc=1, device_id=grp_near()[0], device_id_type=MESH)
 
     @pl.when(me == 0)
     def _():
@@ -157,30 +199,57 @@
                         block = jnp.where(offsets[s - 1] == d, mass_v[g, s], block)
                 band[p, j * bs:(j + 1) * bs, b * bs:(b + 1) * bs] = block
 
-    def product(p, cols):
+    def product(p):
         return jnp.dot(
-            band[p], ctrl_v[pl.ds(p * halo, 3 * halo), cols], preferred_element_type=F32
+            band[p], ctrl_v[pl.ds(pl.multiple_of(p * halo, halo), 3 * halo), :],
+            preferred_element_type=F32,
         ).astype(BF16)
 
     order = row_order(width, lanes, fused)
 
     def turned(p, target, at):
-        block = obs_v[pl.ds(p * halo, halo), :].T
+        block = obs_v[pl.ds(pl.multiple_of(p * halo, halo), halo), :].T
         for source, dest, count in order:
             target[dest:dest + count, at:at + halo] = block[source:source + count, :]
+
+    outer = core * (pairs - 1)
+    inner = (1 - core) * (pairs - 1)
+    inside = pl.multiple_of((1 - core) * halo, halo)
+    beyond = pl.multiple_of(core * 2 * halo, halo)
+    outer_row = pl.multiple_of(outer * halo, halo)
 
     loads[1].wait()
     loads[3].wait()
     for p in range(1, pairs - 1):
         build(p)
-        mc_in[(p - 1) * halo:p * halo, :] = product(p, slice(0, width))
+        mc_in[(p - 1) * halo:p * halo, :] = product(p)
     build(0)
     build(pairs - 1)
+    mc_local[...] = jnp.dot(
+        band[outer, :, pl.ds(inside, 2 * halo)],
+        ctrl_v[pl.ds(outer_row + inside, 2 * halo), :],
+        preferred_element_type=F32,
+    )
     loads[2].wait()
     for p in range(1, pairs - 1):
         turned(p, obs_in, (p - 1) * halo)
-    turned(0, obs_edge, 0)
-    turned(pairs - 1, obs_edge, halo)
+    turned(inner, obs_in, (pairs - 2) * halo)
+    turned(outer, obs_edge, 0)
+    for step in range(steps - 1):
+        hear_z(step)
+        tell_z(step + 1)
+
+    @pl.when(core == 0)
+    def _():
+        for h in range(CHUNKS):
+            to_left(h).wait_recv()
+
+    @pl.when(core == 1)
+    def _():
+        for h in range(CHUNKS):
+            to_right(h).wait_recv()
+
+    mc_in[(pairs - 2) * halo:(pairs - 1) * halo, :] = product(inner)
     half = width // 2
     for r in range(2):
         gram[r * half:(r + 1) * half, :] = jnp.dot(
@@ -188,17 +257,22 @@
         )
 
     def edges(h):
-        @pl.when(me > 0)
+        @pl.when((me > 0) & (core == 0))
         def _():
             to_right(h).wait_recv()
 
-        mc_edge[0:halo, chunks[h]] = product(0, chunks[h])
-
-        @pl.when(me < last)
+        @pl.when((me < last) & (core == 1))
         def _():
             to_left(h).wait_recv()
 
-        mc_edge[halo:2 * halo, chunks[h]] = product(pairs - 1, chunks[h])
+        mc_edge[:, chunks[h]] = (
+            mc_local[:, chunks[h]]
+            + jnp.dot(
+                band[outer, :, pl.ds(beyond, halo)],
+                ctrl_v[pl.ds(outer_row + beyond, halo), chunks[h]],
+                preferred_element_type=F32,
+            )
+        ).astype(BF16)
 
     def finished(start, count, cols):
         return gram[pl.ds(start, count), cols] + jnp.dot(
@@ -255,6 +329,8 @@
 
     def stage_core(h):
         copy_a(h).wait_recv()
+        if h == 0 and steps > 0:
+            hear_z(steps - 1)
         total = gram[pl.ds(mine, half), chunks[h]] + recv_a[h]
         gram[pl.ds(mine, half), chunks[h]] = total
         send_z[h] = total.astype(BF16).reshape(zs, piece, chunk)
@@ -278,6 +354,8 @@
             total = total + gath[h, k].astype(F32)
         out_ref[:, chunks[h]] = total
 
+    if groups == 4:
+        pl.semaphore_wait(tok_g, 1)
     for h in range(CHUNKS):
         stage_edges(h)
         if h >= 1:
@@ -322,10 +400,11 @@
                 pltpu.VMEM((rows, width), BF16),
                 pltpu.VMEM((nblk, slots, bs, bs), BF16),
                 pltpu.VMEM((pairs, halo, 3 * halo), BF16),
-                pltpu.VMEM((width, rows - 2 * halo), BF16),
-                pltpu.VMEM((width, 2 * halo), BF16),
-                pltpu.VMEM((rows - 2 * halo, width), BF16),
-                pltpu.VMEM((2 * halo, width), BF16),
+                pltpu.VMEM((width, rows - halo), BF16),
+                pltpu.VMEM((width, halo), BF16),
+                pltpu.VMEM((rows - halo, width), BF16),
+                pltpu.VMEM((halo, width), F32),
+                pltpu.VMEM((halo, width), BF16),
                 pltpu.VMEM((width, width), F32),
                 pltpu.VMEM((CHUNKS, half, chunk), F32),
                 pltpu.VMEM((CHUNKS, half, chunk), F32),
@@ -335,6 +414,7 @@
                 dma((4,)), dma((2, CHUNKS)), dma((2, CHUNKS)), dma((CHUNKS,)), dma((CHUNKS,)),
                 dma((CHUNKS, zs - 1)), dma((CHUNKS, zs - 1)),
                 dma((CHUNKS, groups - 1)), dma((CHUNKS, groups - 1)),
+                pltpu.SemaphoreType.REGULAR((2, max(zs - 2, 1))), pltpu.SemaphoreType.REGULAR,
             ],
             compiler_params=pltpu.CompilerParams(
                 collective_id=0, has_side_effects=True, vmem_limit_bytes=56 * 2**20

time: 24.5 us -> 24 us (0.980)
  Pallas kernels: 23.7 us -> 23.2 us
    pallas_call x1, Pallas kernels: 23.7 us -> 23.2 us  [shards(): pl.pallas_call(functools.partial(kernel, groups, lanes, fused, nblk, bs),...]
where the time goes in v2:
time: 24 us; the launch traced here: 23.8 us
  Pallas kernels  23.2 us (97%)
  local copies, waits for them, and re-layouts  0.66 us (3%)
    pallas_call x1, Pallas kernels, shards(): pl.pallas_call(functools.partial(kernel, groups, lanes, fused, nblk, bs),...  23.2 us
    unnamed x1, local copies, waits for them, and re-layouts  0.66 us

profile of v2, /device:TPU:0, one launch (start us, length us, event | category | flops | bytes accessed | tf_op | source)
XLA Modules:
  0.0 23.8 jit_solution(4449639906782697781)
XLA Ops:
  0.0 23.2 %shard_map.46 = f32[64,512]{1,0:T(8,128)S(1)} custom-call(s32[4,12]{1,0:T(4,128)} %bitcast.1, bf16[1536,512]{1,0:T(8,128)(2,1)} %ctrl_hbm.1, bf16[1536,512]{1,0:T(8,128)(2,1)} %obs_hbm.1, bf16[12,4,128,128]{3,2,1,0:T(8,128)(2,1)} %mass_hbm.1), custom_call_target="tpu_custom_call" | custom-call | tf_op jit(solution)/shard_map/pallas_call | solution.py:392
  23.2 0.7 %copy.6 = f32[64,512]{1,0:T(8,128)} copy(f32[64,512]{1,0:T(8,128)S(1)} %shard_map.46) | data formatting | bytes 262144
